TPU v7x, 32 devices: a whole 2x2x4 slice. The times are simulated.
32 devices in a mesh: section: 2 (over core), tensor: 4 (over z), dp: 4 (over y, x).
Axes of the slice: x: 2, y: 2, z: 4, core: 2. Of those that a mesh axis runs over, the one named last changes fastest.
Arguments:
- block_input: bfloat16 [8, 256, 2048], P('dp'), may hold values from -6 to 6
- cotangent: bfloat16 [8, 256, 2048], P('dp'), may hold values from -6 to 6
- lengths: int32 [8], P('dp'), may hold values from 1 to 256, 1280 in all
- attn_norm: bfloat16 [2, 2048], P('section', 'dp'), may hold values from 0.5 to 1.5
- w_qkv: bfloat16 [2, 2048, 3, 2048], P('section', 'dp', None, 'tensor')
- w_out: bfloat16 [2, 2048, 2048], P('section', 'tensor', 'dp'), may hold values from -0.5 to 0.5
- mlp_norm: bfloat16 [2, 2048], P('section', 'dp'), may hold values from 0.5 to 1.5
- w_gate_up: bfloat16 [2, 2048, 2, 8192], P('section', 'dp', None, 'tensor'), may hold values from -0.125 to 0.125
- w_down: bfloat16 [2, 8192, 2048], P('section', 'tensor', 'dp'), may hold values from -0.0625 to 0.0625
Outputs:
- activations: bfloat16 [2, 8, 256, 2048], P('section', 'dp')
- input_grads: bfloat16 [2, 8, 256, 2048], P('section', 'dp')
- grad_attn_norm: float32 [2, 2048], P('section', 'dp')
- grad_qkv: float32 [2, 2048, 3, 2048], P('section', 'dp', None, 'tensor')
- grad_out: float32 [2, 2048, 2048], P('section', 'tensor', 'dp')
- grad_mlp_norm: float32 [2, 2048], P('section', 'dp')
- grad_gate_up: float32 [2, 2048, 2, 8192], P('section', 'dp', None, 'tensor')
- grad_down: float32 [2, 8192, 2048], P('section', 'tensor', 'dp')
Inputs may be any that keep to these rules, and one draw needn't show every extreme that they name: lengths[n] counts the real tokens of sequence n, at positions 0 to lengths[n] - 1; the lengths sum to 1280 and the longest is exactly 256.
All inputs are finite; a program needn't handle non-finite values. No bound on the sum of `lengths` on one device may be relied on, other than what follows from the above.
Results may differ from a plain program's by a relative error of at most 0.02.
Values may be sent and summed in bfloat16 or wider, within the bound.
No kernel may reach another device: no remote copies, remote signals or barrier semaphores. Data moves between devices by JAX's collectives and lax.ppermute only.
A program may use at most 320 MiB of HBM per device.

v0:
```python
import jax
import jax.numpy as jnp
from jax import lax
from jax.sharding import PartitionSpec as P

HEAD_DIM = 64


EPSILON = 1e-05
THETA = 130000.0


def from_behind(value, axis, steps):
    count = lax.axis_size(axis)
    leading, last = (max(0, -steps), min(count, count - steps))
    return lax.ppermute(value, axis, [(source, source + steps) for source in range(leading, last)])


def rotary(seq, half):
    position = jnp.arange(seq, dtype=jnp.float32)[:, None]
    exponent = jnp.arange(half, dtype=jnp.float32) * (-1.0 / half)
    angle = position * (THETA**exponent)[None, :]
    return (jnp.cos(angle)[:, None, :], jnp.sin(angle)[:, None, :])


def rotate(values, cosine, sine):
    half = values.shape[-1] // 2
    front, back = (values[..., :half], values[..., half:])
    return jnp.concatenate([front * cosine - back * sine, back * cosine + front * sine], axis=-1)


def unrotate(grads, cosine, sine):
    half = grads.shape[-1] // 2
    front, back = (grads[..., :half], grads[..., half:])
    return jnp.concatenate([front * cosine + back * sine, back * cosine - front * sine], axis=-1)


def normalize(resid, gain):
    inverse = lax.rsqrt(jnp.mean(resid * resid, axis=-1, keepdims=True) + EPSILON)
    normed = resid * inverse
    return (normed, inverse, normed * gain.astype(jnp.float32))


def forward_parts(weights, inputs, length):
    gain_one, w_qkv, w_out, gain_two, w_gate_up, w_down = weights
    seq, width = inputs.shape
    local = w_qkv.shape[2]
    heads = local // HEAD_DIM
    units = w_gate_up.shape[2]
    scale = HEAD_DIM ** (-0.5)
    resid = inputs.astype(jnp.float32)
    normed_one, inverse_one, scaled_one = normalize(resid, gain_one)
    attn_in = scaled_one.astype(jnp.bfloat16)
    proj = jnp.dot(attn_in, w_qkv.reshape(width, 3 * local), preferred_element_type=jnp.float32)
    proj = proj.reshape(seq, 3, heads, HEAD_DIM)
    cosine, sine = rotary(seq, HEAD_DIM // 2)
    query = rotate(proj[:, 0], cosine, sine).astype(jnp.bfloat16)
    keys = rotate(proj[:, 1], cosine, sine).astype(jnp.bfloat16)
    values = proj[:, 2].astype(jnp.bfloat16)
    scores = jnp.einsum("qhd,khd->hqk", query, keys, preferred_element_type=jnp.float32) * scale
    position = jnp.arange(seq, dtype=jnp.int32)
    allowed = (position[None, :] <= position[:, None]) & (position[None, :] < length)
    masked = jnp.where(allowed[None], scores, -1e30)
    top = jnp.max(masked, axis=-1, keepdims=True)
    logsum = top + jnp.log(jnp.sum(jnp.exp(masked - top), axis=-1, keepdims=True))
    probs = jnp.where(allowed[None], jnp.exp(masked - logsum), 0.0).astype(jnp.bfloat16)
    attended = jnp.einsum("hqk,khd->qhd", probs, values, preferred_element_type=jnp.float32)
    attended = attended.astype(jnp.bfloat16).reshape(seq, local)
    attn_part = jnp.dot(attended, w_out, preferred_element_type=jnp.float32)
    hidden = resid + lax.psum(attn_part, "tensor")
    normed_two, inverse_two, scaled_two = normalize(hidden, gain_two)
    mlp_in = scaled_two.astype(jnp.bfloat16)
    pair = jnp.dot(mlp_in, w_gate_up.reshape(width, 2 * units), preferred_element_type=jnp.float32)
    pair = pair.reshape(seq, 2, units)
    gate, upper = (pair[:, 0], pair[:, 1])
    mixed = (jax.nn.silu(gate) * upper).astype(jnp.bfloat16)
    down_part = jnp.dot(mixed, w_down, preferred_element_type=jnp.float32)
    valid = (position < length)[:, None]
    output = jnp.where(valid, hidden + lax.psum(down_part, "tensor"), 0.0)
    return {
        "normed_one": normed_one,
        "inverse_one": inverse_one,
        "attn_in": attn_in,
        "query": query,
        "keys": keys,
        "values": values,
        "probs": probs,
        "attended": attended,
        "normed_two": normed_two,
        "inverse_two": inverse_two,
        "mlp_in": mlp_in,
        "gate": gate,
        "upper": upper,
        "mixed": mixed,
        "valid": valid,
        "cosine": cosine,
        "sine": sine,
        "output": output.astype(jnp.bfloat16),
    }


def backward_parts(weights, inputs, length, upstream):
    gain_one, w_qkv, w_out, gain_two, w_gate_up, w_down = weights
    parts = forward_parts(weights, inputs, length)
    seq = inputs.shape[0]
    local = w_qkv.shape[2]
    heads = local // HEAD_DIM
    scale = HEAD_DIM ** (-0.5)
    grad_y = jnp.where(parts["valid"], upstream.astype(jnp.float32), 0.0)
    grad_yb = grad_y.astype(jnp.bfloat16)
    grad_down = jnp.dot(parts["mixed"].T, grad_yb, preferred_element_type=jnp.float32)
    grad_mixed = jnp.dot(grad_yb, w_down.T, preferred_element_type=jnp.float32)
    gate, upper = (parts["gate"], parts["upper"])
    sigma = jax.nn.sigmoid(gate)
    grad_gate = grad_mixed * upper * sigma * (1.0 + gate * (1.0 - sigma))
    grad_upper = grad_mixed * gate * sigma
    grad_pair = jnp.stack([grad_gate, grad_upper], axis=1).astype(jnp.bfloat16)
    grad_gate_up = jnp.einsum(
        "ld,lcf->dcf", parts["mlp_in"], grad_pair, preferred_element_type=jnp.float32
    )
    mlp_part = jnp.einsum("lcf,dcf->ld", grad_pair, w_gate_up, preferred_element_type=jnp.float32)
    grad_mlp_in = lax.psum(mlp_part, "tensor")
    normed_two = parts["normed_two"]
    grad_gain_two = jnp.sum(grad_mlp_in * normed_two, axis=0)
    through_two = grad_mlp_in * gain_two.astype(jnp.float32)
    grad_hidden = grad_y + parts["inverse_two"] * (
        through_two - normed_two * jnp.mean(through_two * normed_two, axis=-1, keepdims=True)
    )
    grad_hb = grad_hidden.astype(jnp.bfloat16)
    grad_w_out = jnp.dot(parts["attended"].T, grad_hb, preferred_element_type=jnp.float32)
    grad_att = jnp.dot(grad_hb, w_out.T, preferred_element_type=jnp.float32).astype(jnp.bfloat16)
    grad_att = grad_att.reshape(seq, heads, HEAD_DIM)
    probs = parts["probs"]
    attended = parts["attended"].reshape(seq, heads, HEAD_DIM)
    grad_value = jnp.einsum(
        "hqk,qhd->khd", probs, grad_att, preferred_element_type=jnp.float32
    ).astype(jnp.bfloat16)
    grad_probs = jnp.einsum(
        "qhd,khd->hqk", grad_att, parts["values"], preferred_element_type=jnp.float32
    )
    delta = jnp.einsum("qhd,qhd->hq", grad_att, attended, preferred_element_type=jnp.float32)[
        ..., None
    ]
    grad_scores = (probs.astype(jnp.float32) * (grad_probs - delta) * scale).astype(jnp.bfloat16)
    query_raw = jnp.einsum(
        "hqk,khd->qhd", grad_scores, parts["keys"], preferred_element_type=jnp.float32
    )
    key_raw = jnp.einsum(
        "hqk,qhd->khd", grad_scores, parts["query"], preferred_element_type=jnp.float32
    )
    grad_query = unrotate(query_raw, parts["cosine"], parts["sine"]).astype(jnp.bfloat16)
    grad_key = unrotate(key_raw, parts["cosine"], parts["sine"]).astype(jnp.bfloat16)
    grad_proj = jnp.stack([grad_query, grad_key, grad_value], axis=1).reshape(seq, 3, local)
    grad_w_qkv = jnp.einsum(
        "ld,lcj->dcj", parts["attn_in"], grad_proj, preferred_element_type=jnp.float32
    )
    attn_part = jnp.einsum("lcj,dcj->ld", grad_proj, w_qkv, preferred_element_type=jnp.float32)
    grad_attn_in = lax.psum(attn_part, "tensor")
    normed_one = parts["normed_one"]
    grad_gain_one = jnp.sum(grad_attn_in * normed_one, axis=0)
    through_one = grad_attn_in * gain_one.astype(jnp.float32)
    grad_input = grad_hidden + parts["inverse_one"] * (
        through_one - normed_one * jnp.mean(through_one * normed_one, axis=-1, keepdims=True)
    )
    grads = (grad_gain_one, grad_w_qkv, grad_w_out, grad_gain_two, grad_gate_up, grad_down)
    return (grad_input.astype(jnp.bfloat16), grads)


def add_tuples(total, extra):
    if total is None:
        return extra
    return tuple((left + right for left, right in zip(total, extra)))


def per_device(
    block_input, cotangent, lengths, attn_norm, w_qkv, w_out, mlp_norm, w_gate_up, w_down
):
    micro = block_input.shape[0]
    first = lax.axis_index("section") == 0
    shards = (attn_norm[0], w_qkv[0], w_out[0], mlp_norm[0], w_gate_up[0], w_down[0])
    weights = (
        lax.all_gather(shards[0], "dp", axis=0, tiled=True),
        lax.all_gather(shards[1], "dp", axis=0, tiled=True),
        lax.all_gather(shards[2], "dp", axis=1, tiled=True),
        lax.all_gather(shards[3], "dp", axis=0, tiled=True),
        lax.all_gather(shards[4], "dp", axis=0, tiled=True),
        lax.all_gather(shards[5], "dp", axis=1, tiled=True),
    )
    blank = jnp.zeros_like(block_input[0])
    received = []
    outputs = []
    for tick in range(micro + 1):
        early = min(tick, micro - 1)
        late = max(tick - 1, 0)
        upstream = received[tick - 1] if tick >= 1 else blank
        tick_in = jnp.where(first, block_input[early], upstream)
        tick_len = jnp.where(first, lengths[early], lengths[late])
        result = forward_parts(weights, tick_in, tick_len)["output"]
        outputs.append(result)
        if tick < micro:
            received.append(from_behind(result, "section", 1))
    kept_inputs = [jnp.where(first, block_input[index], received[index]) for index in range(micro)]
    activations = jnp.stack(
        [jnp.where(first, outputs[index], outputs[index + 1]) for index in range(micro)]
    )[None]
    weights = (
        lax.all_gather(shards[0], "dp", axis=0, tiled=True),
        lax.all_gather(shards[1], "dp", axis=0, tiled=True),
        lax.all_gather(shards[2], "dp", axis=1, tiled=True),
        lax.all_gather(shards[3], "dp", axis=0, tiled=True),
        lax.all_gather(shards[4], "dp", axis=0, tiled=True),
        lax.all_gather(shards[5], "dp", axis=1, tiled=True),
    )
    totals = None
    returned = []
    grad_ticks = []
    for tick in range(micro + 1):
        early = min(tick, micro - 1)
        late = max(tick - 1, 0)
        tick_in = jnp.where(first, kept_inputs[late], kept_inputs[early])
        tick_len = jnp.where(first, lengths[late], lengths[early])
        downstream = returned[tick - 1] if tick >= 1 else blank
        incoming = jnp.where(first, downstream, cotangent[early])
        active = jnp.where(first, tick >= 1, tick < micro)
        incoming = jnp.where(active, incoming, jnp.zeros_like(incoming))
        grad_in, grads = backward_parts(weights, tick_in, tick_len, incoming)
        totals = add_tuples(totals, grads)
        grad_ticks.append(grad_in)
        if tick < micro:
            returned.append(from_behind(grad_in, "section", -1))
    totals = (
        lax.psum_scatter(totals[0], "dp", scatter_dimension=0, tiled=True),
        lax.psum_scatter(totals[1], "dp", scatter_dimension=0, tiled=True),
        lax.psum_scatter(totals[2], "dp", scatter_dimension=1, tiled=True),
        lax.psum_scatter(totals[3], "dp", scatter_dimension=0, tiled=True),
        lax.psum_scatter(totals[4], "dp", scatter_dimension=0, tiled=True),
        lax.psum_scatter(totals[5], "dp", scatter_dimension=1, tiled=True),
    )
    input_grads = jnp.stack(
        [jnp.where(first, grad_ticks[index + 1], grad_ticks[index]) for index in range(micro)]
    )[None]
    return (
        activations,
        input_grads,
        totals[0][None],
        totals[1][None],
        totals[2][None],
        totals[3][None],
        totals[4][None],
        totals[5][None],
    )


def solution(mesh):
    return jax.shard_map(
        per_device,
        mesh=mesh,
        in_specs=(
            P("dp", None, None),
            P("dp", None, None),
            P("dp"),
            P("section", "dp"),
            P("section", "dp", None, "tensor"),
            P("section", "tensor", "dp"),
            P("section", "dp"),
            P("section", "dp", None, "tensor"),
            P("section", "tensor", "dp"),
        ),
        out_specs=(
            P("section", "dp", None, None),
            P("section", "dp", None, None),
            P("section", "dp"),
            P("section", "dp", None, "tensor"),
            P("section", "tensor", "dp"),
            P("section", "dp"),
            P("section", "dp", None, "tensor"),
            P("section", "tensor", "dp"),
        ),
        check_vma=False,
    )
```

profile of v0, /device:TPU:0, one launch (start us, length us, event | category | flops | bytes accessed | tf_op | source)
XLA Modules:
  0.0 2405.2 jit_solution(1318705741337266363)
XLA Ops:
  20.4 62.2 %all-gather.11.cloned.1.call-done = bf16[1,2048,3,512]{3,1,2,0:T(8,128)(2,1)} async-done(((bf16[1,512,3,512]{3,1,2,0:T(8,128)(2,1)}), bf16[1,2048,3,512]{3,1,2,0:T(8,128)(2,1)}) %all-gather.11.cloned.1.call-update) | async-done | bytes 6291472 | tf_op jit(solution)/shard_map/all_gather | solution.py:183
  98.0 21.6 all-gather.13.cloned.1.call-done
  138.3 71.2 %all-reduce.18.cloned.1.call-done = f32[256,2048]{1,0:T(8,128)} async-done(((f32[256,2048]{1,0:T(8,128)}), f32[256,2048]{1,0:T(8,128)}) %all-reduce.18.cloned.1.call-update) | async-done | bytes 2097168 | tf_op jit(solution)/shard_map/psum | solution.py:70
  211.5 156.6 %all-gather.15.cloned.1.call-done = bf16[1,2048,2,2048]{3,1,2,0:T(8,128)(2,1)} async-done(((bf16[1,512,2,2048]{3,1,2,0:T(8,128)(2,1)}), bf16[1,2048,2,2048]{3,1,2,0:T(8,128)(2,1)}) %all-gather.15.cloned.1.call-update) | async-done | bytes 16777232 | tf_op jit(solution)/shard_map/all_gather | solution.py:186
  368.1 22.8 copy.99
  404.0 53.2 %all-gather.17.cloned.1.call-done = bf16[1,2048,2048]{2,1,0:T(8,128)(2,1)} async-done(((bf16[1,2048,512]{2,1,0:T(8,128)(2,1)}), bf16[1,2048,2048]{2,1,0:T(8,128)(2,1)}) %all-gather.17.cloned.1.call-update) | async-done | bytes 8388624 | tf_op jit(solution)/shard_map/all_gather | solution.py:187
  465.6 86.3 %all-reduce.20.cloned.1.call-done = f32[256,2048]{1,0:T(8,128)} async-done(((f32[256,2048]{1,0:T(8,128)}), f32[256,2048]{1,0:T(8,128)}) %all-reduce.20.cloned.1.call-update) | async-done | bytes 2097168 | tf_op jit(solution)/shard_map/psum | solution.py:79
  578.6 154.1 %all-reduce.34.cloned.1.call-done = (f32[256,2048]{1,0:T(8,128)}, f32[256,2048]{1,0:T(8,128)}) async-done(((f32[256,2048]{1,0:T(8,128)}, f32[256,2048]{1,0:T(8,128)}), (f32[256,2048]{1,0:T(8,128)}, f32[256,2048]{1,0:T(8,128)})) %all-reduce.34.cloned.1.call-update) | async-done | bytes 4194320 | tf_op jit(solution)/shard_map/psum | solution.py:70
  794.1 152.1 %all-reduce.32.cloned.1.call-done = (f32[256,2048]{1,0:T(8,128)}, f32[256,2048]{1,0:T(8,128)}) async-done(((f32[256,2048]{1,0:T(8,128)}, f32[256,2048]{1,0:T(8,128)}), (f32[256,2048]{1,0:T(8,128)}, f32[256,2048]{1,0:T(8,128)})) %all-reduce.32.cloned.1.call-update) | async-done | bytes 4194320 | tf_op jit(solution)/shard_map/psum | solution.py:79
  991.2 154.3 %all-reduce.30.cloned.1.call-done = (f32[256,2048]{1,0:T(8,128)}, f32[256,2048]{1,0:T(8,128)}) async-done(((f32[256,2048]{1,0:T(8,128)}, f32[256,2048]{1,0:T(8,128)}), (f32[256,2048]{1,0:T(8,128)}, f32[256,2048]{1,0:T(8,128)})) %all-reduce.30.cloned.1.call-update) | async-done | bytes 4194320 | tf_op jit(solution)/shard_map/psum | solution.py:158
  1199.3 77.1 %all-reduce.22.cloned.1.call-done = f32[256,2048]{1,0:T(8,128)} async-done(((f32[256,2048]{1,0:T(8,128)}), f32[256,2048]{1,0:T(8,128)}) %all-reduce.22.cloned.1.call-update) | async-done | bytes 2097168 | tf_op jit(solution)/shard_map/psum | solution.py:122
  1310.4 154.1 %all-reduce.28.cloned.1.call-done = (f32[256,2048]{1,0:T(8,128)}, f32[256,2048]{1,0:T(8,128)}) async-done(((f32[256,2048]{1,0:T(8,128)}, f32[256,2048]{1,0:T(8,128)}), (f32[256,2048]{1,0:T(8,128)}, f32[256,2048]{1,0:T(8,128)})) %all-reduce.28.cloned.1.call-update) | async-done | bytes 4194320 | tf_op jit(solution)/shard_map/psum | solution.py:70
  1512.3 18.1 fusion.128
  1537.5 60.8 %all-reduce.24.cloned.1.call-done = f32[256,2048]{1,0:T(8,128)} async-done(((f32[256,2048]{1,0:T(8,128)}), f32[256,2048]{1,0:T(8,128)}) %all-reduce.24.cloned.1.call-update) | async-done | bytes 2097168 | tf_op jit(solution)/shard_map/psum | solution.py:122
  1616.8 18.3 fusion.127
  1635.1 34.7 %add_add_fusion = f32[2048,2,2048]{2,0,1:T(8,128)} fusion(f32[2048,2,2048]{2,0,1:T(8,128)} %fusion.128, f32[2048,2,2048]{2,0,1:T(8,128)} %fusion.127, bf16[256,1,2048]{2,0,1:T(8,128)(2,1)} %get-tuple-element.74, bf16[256,1,2048]{2,0,1:T(8,128)(2,1)S(1)} %copy-done.51, f32[256,2048]{1,0:T(8,128)S(1)} %copy-done.2, f32[256]{0:T(256)S(1)} %add_rsqrt_fusion.4, ...), kind=kOutput, calls=%fused_computation | convolution fusion | flops 4317511680 | bytes 104866816 | tf_op jit(solution)/shard_map/ld,lcf->dcf/dot_general | solution.py:118
  1728.6 20.9 add_add_fusion.1
  1751.4 19.0 all-reduce.26.cloned.1.call-done
  1772.7 17.0 all-reduce.2
  1798.4 262.6 %reduce-scatter.9.cloned.1.call-done = f32[512,2,2048]{2,0,1:T(8,128)} async-done(((f32[2048,2,2048]{2,0,1:T(8,128)}), f32[512,2,2048]{2,0,1:T(8,128)}) %reduce-scatter.9.cloned.1.call-update) | async-done | bytes 8388624 | tf_op jit(solution)/shard_map/reduce_scatter | solution.py:236
  2061.0 15.4 copy.134
  2076.4 40.7 %reduce-scatter.7.cloned.1.call-done = f32[512,512]{1,0:T(8,128)} async-done(((f32[512,2048]{1,0:T(8,128)}), f32[512,512]{1,0:T(8,128)}) %reduce-scatter.7.cloned.1.call-update) | async-done | bytes 1048592 | tf_op jit(solution)/shard_map/reduce_scatter | solution.py:234
  2117.0 124.2 %reduce-scatter.5.cloned.1.call-done = f32[512,3,512]{2,0,1:T(8,128)} async-done(((f32[2048,3,512]{2,0,1:T(8,128)}), f32[512,3,512]{2,0,1:T(8,128)}) %reduce-scatter.5.cloned.1.call-update) | async-done | bytes 3145744 | tf_op jit(solution)/shard_map/reduce_scatter | solution.py:233
  2241.2 157.2 %reduce-scatter.11.cloned.1.call-done = f32[2048,512]{1,0:T(8,128)} async-done(((f32[2048,2048]{1,0:T(8,128)}), f32[2048,512]{1,0:T(8,128)}) %reduce-scatter.11.cloned.1.call-update) | async-done | bytes 4194320 | tf_op jit(solution)/shard_map/reduce_scatter | solution.py:237
  (461 shorter events, 431.6 us)
Async XLA Ops:
  7.2 75.4 %all-gather.11.cloned.1.call-start = ((), (), s32[]{:S(2)}) async-start(), calls=%async_computation.12 | async-start | bytes 7864320 | tf_op jit(solution)/shard_map/all_gather | solution.py:183
  7.9 111.6 %all-gather.13.cloned.1.call-start = ((), (), s32[]{:S(2)}) async-start(), calls=%async_computation.13 | async-start | bytes 2621440 | tf_op jit(solution)/shard_map/all_gather | solution.py:184
  8.7 200.8 %all-reduce.18.cloned.1.call-start = ((), (), s32[]{:S(2)}) async-start(), calls=%async_computation.4 | async-start | bytes 4194304 | tf_op jit(solution)/shard_map/psum | solution.py:70
  19.7 752.1 %copy-start.104 = (pred[256]{0:T(512)(128)(4,1)}, pred[256]{0:T(512)(128)(4,1)S(1)}, u32[]{:S(2)}) copy-start(pred[256]{0:T(512)(128)(4,1)S(1)} %iota_compare_fusion.4) | copy-start | bytes 772
  123.2 244.9 %all-gather.15.cloned.1.call-start = ((), (), s32[]{:S(2)}) async-start(), calls=%async_computation.14 | async-start | bytes 20971520 | tf_op jit(solution)/shard_map/all_gather | solution.py:186
  129.4 327.8 %all-gather.17.cloned.1.call-start = ((), (), s32[]{:S(2)}) async-start(), calls=%async_computation.15 | async-start | bytes 10485760 | tf_op jit(solution)/shard_map/all_gather | solution.py:187
  129.9 421.9 %all-reduce.20.cloned.1.call-start = ((), (), s32[]{:S(2)}) async-start(), calls=%async_computation.5 | async-start | bytes 4194304 | tf_op jit(solution)/shard_map/psum | solution.py:79
  465.6 267.1 %all-reduce.34.cloned.1.call-start = ((), (), s32[]{:S(2)}) async-start(), calls=%async_computation.20 | async-start | bytes 8388608 | tf_op jit(solution)/shard_map/psum | solution.py:70
  554.7 4.5 collective-permute-start
  561.5 588.9 %copy-start.5 = (bf16[256,2048]{1,0:T(8,128)(2,1)}, bf16[256,2048]{1,0:T(8,128)(2,1)S(1)}, u32[]{:S(2)}) copy-start(bf16[256,2048]{1,0:T(8,128)(2,1)S(1)} %get-tuple-element.70) | copy-start | bytes 3145732
  572.7 392.5 %copy-start.37 = (bf16[8,64,256]{2,1,0:T(8,128)(2,1)}, bf16[8,64,256]{2,1,0:T(8,128)(2,1)S(1)}, u32[]{:S(2)}) copy-start(bf16[8,64,256]{2,1,0:T(8,128)(2,1)S(1)} %convolution_convert_fusion.4) | copy-start | bytes 786436
  578.1 368.1 %all-reduce.32.cloned.1.call-start = ((), (), s32[]{:S(2)}) async-start(), calls=%async_computation.19 | async-start | bytes 8388608 | tf_op jit(solution)/shard_map/psum | solution.py:79
  792.1 353.3 %all-reduce.30.cloned.1.call-start = ((), (), s32[]{:S(2)}) async-start(), calls=%async_computation.18 | async-start | bytes 8388608 | tf_op jit(solution)/shard_map/psum | solution.py:158
  958.5 10.7 collective-permute-start.1
  991.1 285.3 %all-reduce.22.cloned.1.call-start = ((), (), s32[]{:S(2)}) async-start(), calls=%async_computation.6 | async-start | bytes 4194304 | tf_op jit(solution)/shard_map/psum | solution.py:122
  1152.3 14.7 collective-permute-start.2
  1190.3 274.2 %all-reduce.28.cloned.1.call-start = ((), (), s32[]{:S(2)}) async-start(), calls=%async_computation.17 | async-start | bytes 8388608 | tf_op jit(solution)/shard_map/psum | solution.py:70
  1310.3 288.0 %all-reduce.24.cloned.1.call-start = ((), (), s32[]{:S(2)}) async-start(), calls=%async_computation.7 | async-start | bytes 4194304 | tf_op jit(solution)/shard_map/psum | solution.py:122
  1471.3 14.5 collective-permute-start.3
  1511.6 258.7 %all-reduce.26.cloned.1.call-start = ((), (), s32[]{:S(2)}) async-start(), calls=%async_computation.16 | async-start | bytes 8388608 | tf_op jit(solution)/shard_map/psum | solution.py:79
  1616.2 444.8 %reduce-scatter.9.cloned.1.call-start = ((), (), s32[]{:S(2)}) async-start(), calls=%async_computation.10 | async-start | bytes 41943040 | tf_op jit(solution)/shard_map/reduce_scatter | solution.py:236
  1669.8 447.2 %reduce-scatter.7.cloned.1.call-start = ((), (), s32[]{:S(2)}) async-start(), calls=%async_computation.9 | async-start | bytes 5242880 | tf_op jit(solution)/shard_map/reduce_scatter | solution.py:234
  1677.7 563.5 %reduce-scatter.5.cloned.1.call-start = ((), (), s32[]{:S(2)}) async-start(), calls=%async_computation.8 | async-start | bytes 15728640 | tf_op jit(solution)/shard_map/reduce_scatter | solution.py:233
  1708.5 689.9 %reduce-scatter.11.cloned.1.call-start = ((), (), s32[]{:S(2)}) async-start(), calls=%async_computation.11 | async-start | bytes 20971520 | tf_op jit(solution)/shard_map/reduce_scatter | solution.py:237
  (121 other events, 989.1 us)
Sparse Core Ops, SparseCore 0:
  9.9 72.7 all-gather.10
  84.5 35.0 all-gather.12
  123.3 86.1 all-reduce.17
  211.8 156.3 all-gather.14
  369.8 87.3 all-gather.16
  465.7 86.1 all-reduce.19
  578.3 154.4 all-reduce.33
  792.2 153.9 all-reduce.31
  991.3 154.1 all-reduce.29
  1190.4 85.9 all-reduce.21
  1310.4 154.0 all-reduce.27
  1511.8 86.5 all-reduce.23
  1616.3 154.0 all-reduce.25
  1773.3 287.6 reduce-scatter.8
  2064.4 52.5 reduce-scatter.6
  2120.6 120.5 reduce-scatter.4
  2244.7 153.7 reduce-scatter.10
where the time goes:
time: 2410 us
  waiting for transfers between devices  1810 us (75%)
  matrix products  376 us (16%)
  local copies, waits for them, and re-layouts  86.3 us (4%)
  other arithmetic  69.6 us (3%)
  blocking collectives  34.8 us (1%)
    psum x3, waiting for transfers between devices, forward_parts(): hidden = resid + lax.psum(attn_part, 'tensor')  380 us
    reduce_scatter x1, waiting for transfers between devices, per_device(): lax.psum_scatter(totals[4], 'dp', scatter_dimension=0, tiled=True)  263 us
    psum x3, waiting for transfers between devices, forward_parts(): output = jnp.where(valid, hidden + lax.psum(down_part, 'tensor'), 0.0)  257 us
    reduce_scatter x1, waiting for transfers between devices, per_device(): lax.psum_scatter(totals[5], 'dp', scatter_dimension=1, tiled=True)  157 us
    all_gather x1, waiting for transfers between devices, per_device(): lax.all_gather(shards[4], 'dp', axis=0, tiled=True)  157 us
    psum x1, waiting for transfers between devices, backward_parts(): grad_attn_in = lax.psum(attn_part, 'tensor')  154 us
    psum x2, waiting for transfers between devices, backward_parts(): grad_mlp_in = lax.psum(mlp_part, 'tensor')  138 us
    reduce_scatter x1, waiting for transfers between devices, per_device(): lax.psum_scatter(totals[1], 'dp', scatter_dimension=0, tiled=True)  124 us
  transfers between devices with their start and end apart: 21, of which 17 were waited for; matrix products, arithmetic and copies ran while one was open for 12% of the time, Pallas kernels for 0%

commit v1 on v0

v1 whole, which is shorter than its diff:
```python
import jax
import jax.numpy as jnp
from jax import lax
from jax.sharding import PartitionSpec as P

HEAD_DIM = 64
EPSILON = 1e-05
THETA = 130000.0
BF = jnp.bfloat16
F32 = jnp.float32


def swap(value, axis, bits):
    count = lax.axis_size(axis)
    return lax.ppermute(value, axis, [(source, source ^ bits) for source in range(count)])


def mm(left, right, dims):
    return lax.dot_general(left, right, (dims, ((), ())), preferred_element_type=F32)


def reduce_tokens(partial):
    sent = partial.astype(BF)
    half = sent[0].astype(F32)
    for c in range(1, sent.shape[0]):
        half = half + swap(sent[c], "section", c).astype(F32)
    half_b = half.astype(BF)
    total = half[0]
    for k in range(1, half.shape[0]):
        total = total + swap(half_b[k], "tensor", k).astype(F32)
    return total


def gather_tokens(own):
    row = jnp.stack([own] + [swap(own, "tensor", k) for k in range(1, lax.axis_size("tensor"))])
    return jnp.stack([row] + [swap(row, "section", c) for c in range(1, lax.axis_size("section"))])


def normalize(resid, gain):
    inverse = lax.rsqrt(jnp.mean(resid * resid, axis=-1, keepdims=True) + EPSILON)
    normed = resid * inverse
    return normed, inverse, (normed * gain).astype(BF)


def rotate(values, cosine, sine):
    half = values.shape[-1] // 2
    front, back = values[..., :half], values[..., half:]
    return jnp.concatenate([front * cosine - back * sine, back * cosine + front * sine], axis=-1)


def unrotate(grads, cosine, sine):
    half = grads.shape[-1] // 2
    front, back = grads[..., :half], grads[..., half:]
    return jnp.concatenate([front * cosine + back * sine, back * cosine - front * sine], axis=-1)


def attention(proj, cosine, sine, allowed):
    count, seq, _, heads, _ = proj.shape
    query = rotate(proj[:, :, 0], cosine, sine).astype(BF)
    keys = rotate(proj[:, :, 1], cosine, sine).astype(BF)
    values = proj[:, :, 2].astype(BF)
    scores = jnp.einsum("nqhd,nkhd->nhqk", query, keys, preferred_element_type=F32) * HEAD_DIM**-0.5
    masked = jnp.where(allowed, scores, -1e30)
    top = jnp.max(masked, axis=-1, keepdims=True)
    logsum = top + jnp.log(jnp.sum(jnp.exp(masked - top), axis=-1, keepdims=True))
    probs = jnp.where(allowed, jnp.exp(masked - logsum), 0.0).astype(BF)
    attended = jnp.einsum("nhqk,nkhd->nqhd", probs, values, preferred_element_type=F32).astype(BF)
    return query, keys, values, probs, attended


def attention_grad(saved, grad_att, cosine, sine):
    query, keys, values, probs, attended = saved
    grad_value = jnp.einsum("nhqk,nqhd->nkhd", probs, grad_att, preferred_element_type=F32).astype(BF)
    grad_probs = jnp.einsum("nqhd,nkhd->nhqk", grad_att, values, preferred_element_type=F32)
    delta = jnp.einsum("nqhd,nqhd->nhq", grad_att, attended, preferred_element_type=F32)[..., None]
    grad_scores = (probs.astype(F32) * (grad_probs - delta) * HEAD_DIM**-0.5).astype(BF)
    query_raw = jnp.einsum("nhqk,nkhd->nqhd", grad_scores, keys, preferred_element_type=F32)
    key_raw = jnp.einsum("nhqk,nqhd->nkhd", grad_scores, query, preferred_element_type=F32)
    grad_query = unrotate(query_raw, cosine, sine).astype(BF)
    grad_key = unrotate(key_raw, cosine, sine).astype(BF)
    return jnp.stack([grad_query, grad_key, grad_value], axis=2)


def per_device(block_input, cotangent, lengths, attn_norm, w_qkv, w_out, mlp_norm, w_gate_up, w_down):
    section, tensor = lax.axis_index("section"), lax.axis_index("tensor")
    cores, lanes = lax.axis_size("section"), lax.axis_size("tensor")
    micro, seq, width = block_input.shape
    count = micro // cores
    span = seq // lanes
    tokens = micro * seq

    def to_relative(value):
        blocks = value.reshape(cores, count, lanes, span, width)
        rows = []
        for c in range(cores):
            core = lax.dynamic_index_in_dim(blocks, section ^ c, 0, False)
            rows.append(jnp.stack([lax.dynamic_index_in_dim(core, tensor ^ k, 1, False) for k in range(lanes)]))
        return jnp.stack(rows).reshape(cores, lanes, count * span, width)

    def from_relative(value):
        blocks = value.reshape(cores, lanes, count, span, width)
        rows = []
        for c in range(cores):
            core = lax.dynamic_index_in_dim(blocks, section ^ c, 0, False)
            rows.append(jnp.stack([lax.dynamic_index_in_dim(core, tensor ^ k, 0, False) for k in range(lanes)], axis=1))
        return jnp.stack(rows).reshape(micro, seq, width)

    gains = jnp.stack([attn_norm[0], mlp_norm[0]])
    gains = lax.all_gather(lax.all_gather(gains, "dp", axis=1, tiled=True), "section", axis=0).astype(F32)

    def halves(shard, axis):
        shape = shard.shape
        split = shard.reshape(shape[:axis] + (cores, shape[axis] // cores) + shape[axis + 1 :])
        mine = lax.dynamic_index_in_dim(split, section, axis, False)
        other = lax.dynamic_index_in_dim(split, 1 - section, axis, False)
        return mine, swap(other, "section", 1)

    def layers_of(mine, got):
        return jnp.where(section == 0, mine, got), jnp.where(section == 0, got, mine)

    rows = w_qkv.shape[1]
    qkv = layers_of(*halves(w_qkv[0], 2))
    out = layers_of(*halves(w_out[0], 0))
    gate_up = layers_of(*halves(w_gate_up[0], 2))
    down = layers_of(*halves(w_down[0], 0))
    local = qkv[0].shape[2]
    units = gate_up[0].shape[2]
    heads = local // HEAD_DIM

    def gathered(layer):
        return (
            lax.all_gather(qkv[layer].reshape(rows, 3 * local), "dp", axis=0, tiled=True),
            lax.all_gather(out[layer], "dp", axis=1, tiled=True),
            lax.all_gather(gate_up[layer].reshape(rows, 2 * units), "dp", axis=0, tiled=True),
            lax.all_gather(down[layer], "dp", axis=1, tiled=True),
        )

    block = (jnp.arange(lanes, dtype=jnp.int32) ^ tensor)[:, None, None]
    step = jnp.arange(span, dtype=jnp.int32)[None, None, :]
    position = jnp.broadcast_to(block * span + step, (lanes, count, span))
    own_lengths = lengths.reshape(cores, count)
    limit = jnp.stack([lax.dynamic_index_in_dim(own_lengths, section ^ c, 0, False) for c in range(cores)])
    valid = position[None] < limit[:, None, :, None]
    valid = valid.reshape(cores, lanes, count * span, 1)
    flat = position.transpose(1, 0, 2).reshape(count, seq)
    allowed = (flat[None, :, None, :] <= flat[None, :, :, None]) & (flat[None, :, None, :] < limit[:, :, None, None])
    allowed = allowed.reshape(micro, 1, seq, seq)
    exponent = jnp.arange(HEAD_DIM // 2, dtype=F32) * (-2.0 / HEAD_DIM)
    angle = flat.astype(F32)[:, :, None] * (THETA**exponent)
    cosine = jnp.tile(jnp.cos(angle), (cores, 1, 1))[:, :, None, :]
    sine = jnp.tile(jnp.sin(angle), (cores, 1, 1))[:, :, None, :]

    def per_sequence(value):
        inner = value.shape[1:]
        value = value.reshape((cores, lanes, count, span) + inner)
        return value.swapaxes(1, 2).reshape((micro, seq) + inner)

    def per_token(value):
        inner = value.shape[2:]
        value = value.reshape((cores, count, lanes, span) + inner)
        return value.swapaxes(1, 2).reshape((tokens,) + inner)

    def forward(layer, weights, inputs):
        w_qkv, w_out, w_gate_up, w_down = weights
        resid = inputs.astype(F32)
        _, _, attn_in = normalize(resid, gains[layer, 0])
        attn_in = attn_in.reshape(tokens, width)
        proj = mm(attn_in, w_qkv, ((1,), (0,))).reshape(tokens, 3, heads, HEAD_DIM)
        saved = attention(per_sequence(proj), cosine, sine, allowed)
        attended = per_token(saved[-1]).reshape(tokens, local)
        part = mm(attended, w_out, ((1,), (0,)))
        own = resid[0, 0]
        hidden = own + reduce_tokens(part.reshape(inputs.shape))
        normed_two, inverse_two, own_mlp_in = normalize(hidden, gains[layer, 1])
        mlp_in = gather_tokens(own_mlp_in).reshape(tokens, width)
        pair = mm(mlp_in, w_gate_up, ((1,), (0,)))
        gate, upper = pair[:, :units], pair[:, units:]
        mixed = (jax.nn.silu(gate) * upper).astype(BF)
        part = mm(mixed, w_down, ((1,), (0,)))
        output = jnp.where(valid[0, 0], hidden + reduce_tokens(part.reshape(inputs.shape)), 0.0).astype(BF)
        normed_one, inverse_one, _ = normalize(own, gains[layer, 0])
        keep = (attn_in, saved, attended, normed_one, inverse_one, normed_two, inverse_two, mlp_in, gate, upper, mixed)
        return gather_tokens(output), keep

    def scatter(value, axis):
        return lax.psum_scatter(value.astype(BF), "dp", scatter_dimension=axis, tiled=True)

    def backward(layer, weights, keep, upstream):
        w_qkv, w_out, w_gate_up, w_down = weights
        attn_in, saved, attended, normed_one, inverse_one, normed_two, inverse_two, mlp_in, gate, upper, mixed = keep
        grad_y = jnp.where(valid, upstream, jnp.zeros_like(upstream))
        grad_yb = grad_y.reshape(tokens, width)
        grad_down = scatter(mm(mixed, grad_yb, ((0,), (0,))), 1)
        grad_mixed = mm(grad_yb, w_down, ((1,), (1,)))
        sigma = jax.nn.sigmoid(gate)
        grad_gate = grad_mixed * upper * sigma * (1.0 + gate * (1.0 - sigma))
        grad_upper = grad_mixed * gate * sigma
        grad_pair = jnp.concatenate([grad_gate, grad_upper], axis=1).astype(BF)
        part = mm(grad_pair, w_gate_up, ((1,), (1,)))
        grad_gate_up = scatter(mm(mlp_in, grad_pair, ((0,), (0,))), 0)
        grad_mlp_in = reduce_tokens(part.reshape(upstream.shape))
        grad_gain_two = jnp.sum(grad_mlp_in * normed_two, axis=0)
        through = grad_mlp_in * gains[layer, 1]
        grad_hidden = grad_y[0, 0].astype(F32) + inverse_two * (
            through - normed_two * jnp.mean(through * normed_two, axis=-1, keepdims=True)
        )
        grad_hb = gather_tokens(grad_hidden.astype(BF)).reshape(tokens, width)
        grad_att = mm(grad_hb, w_out, ((1,), (1,))).astype(BF)
        grad_out = scatter(mm(attended, grad_hb, ((0,), (0,))), 1)
        grad_att = per_sequence(grad_att.reshape(tokens, heads, HEAD_DIM))
        grad_proj = attention_grad(saved, grad_att, cosine, sine)
        grad_proj = per_token(grad_proj).reshape(tokens, 3 * local)
        part = mm(grad_proj, w_qkv, ((1,), (1,)))
        grad_qkv = scatter(mm(attn_in, grad_proj, ((0,), (0,))), 0)
        grad_attn_in = reduce_tokens(part.reshape(upstream.shape))
        grad_gain_one = jnp.sum(grad_attn_in * normed_one, axis=0)
        through = grad_attn_in * gains[layer, 0]
        grad_input = grad_hidden + inverse_one * (
            through - normed_one * jnp.mean(through * normed_one, axis=-1, keepdims=True)
        )
        grads = (grad_qkv, grad_out, grad_gate_up, grad_down)
        return gather_tokens(grad_input.astype(BF)), grads, jnp.stack([grad_gain_one, grad_gain_two])

    weights = (gathered(0), gathered(1))
    first_out, keep_one = forward(0, weights[0], to_relative(block_input))
    second_out, keep_two = forward(1, weights[1], first_out)
    second_grad, grads_two, gain_grads_two = backward(1, weights[1], keep_two, to_relative(cotangent))
    first_grad, grads_one, gain_grads_one = backward(0, weights[0], keep_one, second_grad)

    activations = from_relative(jnp.where(section == 0, first_out, second_out))[None]
    input_grads = from_relative(jnp.where(section == 0, first_grad, second_grad))[None]

    gain_grads = lax.psum(jnp.stack([gain_grads_one, gain_grads_two]), ("section", "tensor", "dp"))
    gain_grads = lax.dynamic_index_in_dim(gain_grads, section, 0, False)
    gain_grads = lax.dynamic_slice_in_dim(gain_grads, lax.axis_index("dp") * rows, rows, 1)

    def joined(one, two, axis):
        own = jnp.where(section == 0, one, two)
        got = swap(jnp.where(section == 0, two, one), "section", 1)
        low, high = jnp.where(section == 0, own, got), jnp.where(section == 0, got, own)
        return jnp.concatenate([low, high], axis=axis).astype(F32)[None]

    shape_qkv, shape_pair = (rows, 3, local), (rows, 2, units)
    return (
        activations,
        input_grads,
        gain_grads[0][None],
        joined(grads_one[0].reshape(shape_qkv), grads_two[0].reshape(shape_qkv), 2),
        joined(grads_one[1], grads_two[1], 0),
        gain_grads[1][None],
        joined(grads_one[2].reshape(shape_pair), grads_two[2].reshape(shape_pair), 2),
        joined(grads_one[3], grads_two[3], 0),
    )


def solution(mesh):
    return jax.shard_map(
        per_device,
        mesh=mesh,
        in_specs=(
            P("dp", None, None),
            P("dp", None, None),
            P("dp"),
            P("section", "dp"),
            P("section", "dp", None, "tensor"),
            P("section", "tensor", "dp"),
            P("section", "dp"),
            P("section", "dp", None, "tensor"),
            P("section", "tensor", "dp"),
        ),
        out_specs=(
            P("section", "dp", None, None),
            P("section", "dp", None, None),
            P("section", "dp"),
            P("section", "dp", None, "tensor"),
            P("section", "tensor", "dp"),
            P("section", "dp"),
            P("section", "dp", None, "tensor"),
            P("section", "tensor", "dp"),
        ),
        check_vma=False,
    )
```

time: 2410 us -> 1180 us (0.49)
  waiting for transfers between devices: 1810 us -> 652 us
  matrix products: 376 us -> 127 us
  starting transfers between devices: 10.3 us -> 95.5 us
  other arithmetic: 69.6 us -> 112 us
  local copies, waits for them, and re-layouts: 86.3 us -> 116 us
    psum x9 -> x0, waiting for transfers between devices: 929 us -> none  [the longest x3 380 us: forward_parts(): hidden = resid + lax.psum(attn_part, 'tensor')]
    reduce_scatter x4 -> x8, waiting for transfers between devices: 585 us -> 216 us  [scatter(): lax.psum_scatter(value.astype(BF), 'dp', scatter_dimension=axis, tiled=True)]
    ppermute x4 -> x72, waiting for transfers between devices: 0.01 us -> 305 us  [swap(): lax.ppermute(value, axis, [(source, source ^ bits) for source in range(co...]
    dot_general x64 -> x36, matrix products: 376 us -> 127 us  [the longest x24 117 us: mm(): lax.dot_general(left, right, (dims, ((), ())), preferred_element_type=F32)]
    all_gather x4 -> x8, waiting for transfers between devices: 294 us -> 130 us  [the longest x2 87.7 us: gathered(): lax.all_gather(down[layer], 'dp', axis=1, tiled=True)]
    ppermute x4 -> x72, starting transfers between devices: 8.23 us -> 93.2 us  [swap(): lax.ppermute(value, axis, [(source, source ^ bits) for source in range(co...]
    psum x0 -> x1, blocking collectives: none -> 38.5 us  [per_device(): lax.psum(jnp.stack([gain_grads_one, gain_grads_two]), ('section', 'tensor...]
    all_gather x2 -> x0, local copies, waits for them, and re-layouts: 31.5 us -> none  [the longest x1 22.8 us: per_device(): lax.all_gather(shards[4], 'dp', axis=0, tiled=True)]
  transfers between devices with their start and end apart: 21 -> 88, of which waited for: 17 -> 49; matrix products, arithmetic and copies ran while one was open for 12% -> 23% of each run, Pallas kernels for 0% -> 0%
where the time goes in v1:
time: 1180 us; the launch traced here: 1170 us
  waiting for transfers between devices  652 us (55%)
  matrix products  127 us (11%)
  local copies, waits for them, and re-layouts  116 us (10%)
  other arithmetic  112 us (9%)
  starting transfers between devices  95.5 us (8%)
  blocking collectives  49.9 us (4%)
  between operations  16.1 us (1%)
    ppermute x72, waiting for transfers between devices, swap(): lax.ppermute(value, axis, [(source, source ^ bits) for source in range(co...  305 us
    reduce_scatter x8, waiting for transfers between devices, scatter(): lax.psum_scatter(value.astype(BF), 'dp', scatter_dimension=axis, tiled=True)  216 us
    dot_general x24, matrix products, mm(): lax.dot_general(left, right, (dims, ((), ())), preferred_element_type=F32)  117 us
    ppermute x72, starting transfers between devices, swap(): lax.ppermute(value, axis, [(source, source ^ bits) for source in range(co...  93.2 us
    all_gather x2, waiting for transfers between devices, gathered(): lax.all_gather(down[layer], 'dp', axis=1, tiled=True)  87.7 us
    all_gather x2, waiting for transfers between devices, gathered(): lax.all_gather(gate_up[layer].reshape(rows, 2 * units), 'dp', axis=0, til...  40.7 us
    psum x1, blocking collectives, per_device(): lax.psum(jnp.stack([gain_grads_one, gain_grads_two]), ('section', 'tensor...  38.5 us
    unnamed x158, local copies, waits for them, and re-layouts  35 us
  transfers between devices with their start and end apart: 88, of which 49 were waited for; matrix products, arithmetic and copies ran while one was open for 23% of the time, Pallas kernels for 0%

profile of v1, /device:TPU:0, one launch (start us, length us, event | category | flops | bytes accessed | tf_op | source)
XLA Modules:
  0.0 1168.3 jit_solution(2751576315987576266)
XLA Ops:
  22.5 12.1 %reshape_squeeze.14 = bf16[512,2,2,1024]{3,2,1,0:T(2,128)(2,1)} reshape(bf16[1,512,2,2048]{3,2,1,0:T(2,128)(2,1)} %param.16) | data formatting | bytes 8388608 | tf_op jit(solution)/shard_map/reshape;squeeze | solution.py:113
  34.6 11.1 constant_dynamic-slice_fusion.18
  125.0 15.2 %collective-permute-done.4 = bf16[64,2048]{1,0:T(8,128)(2,1)S(1)} collective-permute-done((bf16[64,2048]{1,0:T(8,128)(2,1)}, bf16[64,2048]{1,0:T(8,128)(2,1)S(1)}, u32[]{:S(2)}, u32[]{:S(2)}) %collective-permute-start.4) | collective-permute-done | bytes 262176 | tf_op jit(solution)/shard_map/ppermute | solution.py:15
  153.8 12.1 %collective-permute-done.7 = bf16[64,2048]{1,0:T(8,128)(2,1)S(1)} collective-permute-done((bf16[64,2048]{1,0:T(8,128)(2,1)S(1)}, bf16[64,2048]{1,0:T(8,128)(2,1)S(1)}, u32[]{:S(2)}, u32[]{:S(2)}) %collective-permute-start.7) | collective-permute-done | bytes 262176 | tf_op jit(solution)/shard_map/ppermute | solution.py:15
  170.3 17.5 %all-gather.15.cloned.1.call-done = bf16[2048,2048]{1,0:T(8,128)(2,1)} async-done(((bf16[512,2048]{1,0:T(8,128)(2,1)}), bf16[2048,2048]{1,0:T(8,128)(2,1)}) %all-gather.15.cloned.1.call-update) | async-done | bytes 8388624 | tf_op jit(solution)/shard_map/all_gather | solution.py:134
  198.1 43.9 %all-gather.17.cloned.1.call-done = bf16[1024,2048]{1,0:T(8,128)(2,1)} async-done(((bf16[1024,512]{1,0:T(8,128)(2,1)}), bf16[1024,2048]{1,0:T(8,128)(2,1)}) %all-gather.17.cloned.1.call-update) | async-done | bytes 4194320 | tf_op jit(solution)/shard_map/all_gather | solution.py:135
  261.1 15.0 %collective-permute-done.14 = bf16[64,2048]{1,0:T(8,128)(2,1)S(1)} collective-permute-done((bf16[64,2048]{1,0:T(8,128)(2,1)S(1)}, bf16[64,2048]{1,0:T(8,128)(2,1)S(1)}, u32[]{:S(2)}, u32[]{:S(2)}) %collective-permute-start.14) | collective-permute-done | bytes 262176 | tf_op jit(solution)/shard_map/ppermute | solution.py:15
  287.5 12.3 %collective-permute-done.17 = bf16[64,2048]{1,0:T(8,128)(2,1)S(1)} collective-permute-done((bf16[64,2048]{1,0:T(8,128)(2,1)S(1)}, bf16[64,2048]{1,0:T(8,128)(2,1)S(1)}, u32[]{:S(2)}, u32[]{:S(2)}) %collective-permute-start.17) | collective-permute-done | bytes 262176 | tf_op jit(solution)/shard_map/ppermute | solution.py:15
  336.9 15.4 %collective-permute-done.22 = bf16[64,2048]{1,0:T(8,128)(2,1)S(1)} collective-permute-done((bf16[64,2048]{1,0:T(8,128)(2,1)S(1)}, bf16[64,2048]{1,0:T(8,128)(2,1)S(1)}, u32[]{:S(2)}, u32[]{:S(2)}) %collective-permute-start.22) | collective-permute-done | bytes 262176 | tf_op jit(solution)/shard_map/ppermute | solution.py:15
  363.8 12.6 %collective-permute-done.25 = bf16[64,2048]{1,0:T(8,128)(2,1)S(1)} collective-permute-done((bf16[64,2048]{1,0:T(8,128)(2,1)S(1)}, bf16[64,2048]{1,0:T(8,128)(2,1)S(1)}, u32[]{:S(2)}, u32[]{:S(2)}) %collective-permute-start.25) | collective-permute-done | bytes 262176 | tf_op jit(solution)/shard_map/ppermute | solution.py:15
  381.7 23.2 %all-gather.23.cloned.1.call-done = bf16[2048,2048]{1,0:T(8,128)(2,1)} async-done(((bf16[512,2048]{1,0:T(8,128)(2,1)}), bf16[2048,2048]{1,0:T(8,128)(2,1)}) %all-gather.23.cloned.1.call-update) | async-done | bytes 8388624 | tf_op jit(solution)/shard_map/all_gather | solution.py:134
  415.5 43.8 %all-gather.25.cloned.1.call-done = bf16[1024,2048]{1,0:T(8,128)(2,1)} async-done(((bf16[1024,512]{1,0:T(8,128)(2,1)}), bf16[1024,2048]{1,0:T(8,128)(2,1)}) %all-gather.25.cloned.1.call-update) | async-done | bytes 4194320 | tf_op jit(solution)/shard_map/all_gather | solution.py:135
  487.1 15.0 %collective-permute-done.38 = bf16[64,2048]{1,0:T(8,128)(2,1)S(1)} collective-permute-done((bf16[64,2048]{1,0:T(8,128)(2,1)S(1)}, bf16[64,2048]{1,0:T(8,128)(2,1)S(1)}, u32[]{:S(2)}, u32[]{:S(2)}) %collective-permute-start.38) | collective-permute-done | bytes 262176 | tf_op jit(solution)/shard_map/ppermute | solution.py:15
  515.7 12.3 %collective-permute-done.41 = bf16[64,2048]{1,0:T(8,128)(2,1)S(1)} collective-permute-done((bf16[64,2048]{1,0:T(8,128)(2,1)S(1)}, bf16[64,2048]{1,0:T(8,128)(2,1)S(1)}, u32[]{:S(2)}, u32[]{:S(2)}) %collective-permute-start.41) | collective-permute-done | bytes 262176 | tf_op jit(solution)/shard_map/ppermute | solution.py:15
  577.1 16.3 %collective-permute-done.46 = bf16[64,2048]{1,0:T(8,128)(2,1)S(1)} collective-permute-done((bf16[64,2048]{1,0:T(8,128)(2,1)S(1)}, bf16[64,2048]{1,0:T(8,128)(2,1)S(1)}, u32[]{:S(2)}, u32[]{:S(2)}) %collective-permute-start.46) | collective-permute-done | bytes 262176 | tf_op jit(solution)/shard_map/ppermute | solution.py:15
  617.1 12.2 %collective-permute-done.49 = bf16[64,2048]{1,0:T(8,128)(2,1)S(1)} collective-permute-done((bf16[64,2048]{1,0:T(8,128)(2,1)S(1)}, bf16[64,2048]{1,0:T(8,128)(2,1)S(1)}, u32[]{:S(2)}, u32[]{:S(2)}) %collective-permute-start.49) | collective-permute-done | bytes 262176 | tf_op jit(solution)/shard_map/ppermute | solution.py:15
  662.9 12.2 %collective-permute-done.54 = bf16[64,2048]{1,0:T(8,128)(2,1)S(1)} collective-permute-done((bf16[64,2048]{1,0:T(8,128)(2,1)S(1)}, bf16[64,2048]{1,0:T(8,128)(2,1)S(1)}, u32[]{:S(2)}, u32[]{:S(2)}) %collective-permute-start.54) | collective-permute-done | bytes 262176 | tf_op jit(solution)/shard_map/ppermute | solution.py:15
  687.8 12.3 %collective-permute-done.57 = bf16[64,2048]{1,0:T(8,128)(2,1)} collective-permute-done((bf16[64,2048]{1,0:T(8,128)(2,1)}, bf16[64,2048]{1,0:T(8,128)(2,1)}, u32[]{:S(2)}, u32[]{:S(2)}) %collective-permute-start.57) | collective-permute-done | bytes 262176 | tf_op jit(solution)/shard_map/ppermute | solution.py:15
  795.1 16.3 %collective-permute-done.62 = bf16[64,2048]{1,0:T(8,128)(2,1)S(1)} collective-permute-done((bf16[64,2048]{1,0:T(8,128)(2,1)S(1)}, bf16[64,2048]{1,0:T(8,128)(2,1)S(1)}, u32[]{:S(2)}, u32[]{:S(2)}) %collective-permute-start.62) | collective-permute-done | bytes 262176 | tf_op jit(solution)/shard_map/ppermute | solution.py:15
  848.2 38.5 %psum.7 = f32[2,2,2048]{2,1,0:T(2,128)S(1)} all-reduce(f32[2,2,2048]{2,1,0:T(2,128)S(1)} %pad_maximum_fusion.44), channel_id=1, replica_groups=mesh['section'=2,'tensor'=4,'dp'=4] {'section','tensor','dp'}, use_global_device_ids=true, to_apply=%region_18.19 | all-reduce | flops 8192 | bytes 65536 | tf_op jit(solution)/shard_map/psum | solution.py:233
  898.6 42.9 %reduce-scatter.19.cloned.1.call-done = bf16[512,2048]{1,0:T(8,128)(2,1)} async-done(((bf16[2048,2048]{1,0:T(8,128)(2,1)}), bf16[512,2048]{1,0:T(8,128)(2,1)}) %reduce-scatter.19.cloned.1.call-update) | async-done | bytes 2097168 | tf_op jit(solution)/shard_map/reduce_scatter | solution.py:186
  941.6 89.8 %reduce-scatter.17.cloned.1.call-done = bf16[512,2048]{1,0:T(8,128)(2,1)} async-done(((bf16[2048,2048]{1,0:T(8,128)(2,1)}), bf16[512,2048]{1,0:T(8,128)(2,1)}) %reduce-scatter.17.cloned.1.call-update) | async-done | bytes 2097168 | tf_op jit(solution)/shard_map/reduce_scatter | solution.py:186
  1041.8 36.3 %reduce-scatter.11.cloned.1.call-done = bf16[512,768]{1,0:T(8,128)(2,1)} async-done(((bf16[2048,768]{1,0:T(8,128)(2,1)}), bf16[512,768]{1,0:T(8,128)(2,1)}) %reduce-scatter.11.cloned.1.call-update) | async-done | bytes 786448 | tf_op jit(solution)/shard_map/reduce_scatter | solution.py:186
  1078.2 47.4 %reduce-scatter.9.cloned.1.call-done = bf16[512,768]{1,0:T(8,128)(2,1)} async-done(((bf16[2048,768]{1,0:T(8,128)(2,1)}), bf16[512,768]{1,0:T(8,128)(2,1)}) %reduce-scatter.9.cloned.1.call-update) | async-done | bytes 786448 | tf_op jit(solution)/shard_map/reduce_scatter | solution.py:186
  (538 shorter events, 566.3 us)
Async XLA Ops:
  7.2 82.5 %all-gather.11.cloned.1.call-start = ((), (), s32[]{:S(2)}) async-start(), calls=%async_computation.8 | async-start | bytes 3932160 | tf_op jit(solution)/shard_map/all_gather | solution.py:132
  22.5 79.5 %all-gather.13.cloned.1.call-start = ((), (), s32[]{:S(2)}) async-start(), calls=%async_computation.9 | async-start | bytes 1310720 | tf_op jit(solution)/shard_map/all_gather | solution.py:133
  53.3 134.5 %all-gather.15.cloned.1.call-start = ((), (), s32[]{:S(2)}) async-start(), calls=%async_computation.10 | async-start | bytes 10485760 | tf_op jit(solution)/shard_map/all_gather | solution.py:134
  63.7 178.3 %all-gather.17.cloned.1.call-start = ((), (), s32[]{:S(2)}) async-start(), calls=%async_computation.11 | async-start | bytes 5242880 | tf_op jit(solution)/shard_map/all_gather | solution.py:135
  69.5 231.4 %all-gather.19.cloned.1.call-start = ((), (), s32[]{:S(2)}) async-start(), calls=%async_computation.12 | async-start | bytes 3932160 | tf_op jit(solution)/shard_map/all_gather | solution.py:132
  77.9 237.7 %all-gather.21.cloned.1.call-start = ((), (), s32[]{:S(2)}) async-start(), calls=%async_computation.13 | async-start | bytes 1310720 | tf_op jit(solution)/shard_map/all_gather | solution.py:133
  106.5 298.4 %all-gather.23.cloned.1.call-start = ((), (), s32[]{:S(2)}) async-start(), calls=%async_computation.14 | async-start | bytes 10485760 | tf_op jit(solution)/shard_map/all_gather | solution.py:134
  122.3 336.9 %all-gather.25.cloned.1.call-start = ((), (), s32[]{:S(2)}) async-start(), calls=%async_computation.15 | async-start | bytes 5242880 | tf_op jit(solution)/shard_map/all_gather | solution.py:135
  320.0 526.7 %reduce-scatter.15.cloned.1.call-start = ((), (), s32[]{:S(2)}) async-start(), calls=%async_computation.19 | async-start | bytes 1310720 | tf_op jit(solution)/shard_map/reduce_scatter | solution.py:186
  564.0 39.7 %collective-permute-start.30 = (bf16[64,2048]{1,0:T(8,128)(2,1)S(1)}, bf16[64,2048]{1,0:T(8,128)(2,1)S(1)}, u32[]{:S(2)}, u32[]{:S(2)}) collective-permute-start(bf16[64,2048]{1,0:T(8,128)(2,1)S(1)} %get-tuple-element.155), channel_id=1, source_target_pairs={{0,8},{4,12},{8,0},{12,4},{1,9},{5,13},{9,1},{13,5},{2,10},{6,14},... | collective-permute-start | bytes 786440 | tf_op jit(solution)/shard_map/ppermute | solution.py:15
  682.7 164.0 %reduce-scatter.13.cloned.1.call-start = ((), (), s32[]{:S(2)}) async-start(), calls=%async_computation.18 | async-start | bytes 1310720 | tf_op jit(solution)/shard_map/reduce_scatter | solution.py:186
  707.4 188.8 %reduce-scatter.23.cloned.1.call-start = ((), (), s32[]{:S(2)}) async-start(), calls=%async_computation.23 | async-start | bytes 5242880 | tf_op jit(solution)/shard_map/reduce_scatter | solution.py:186
  713.9 182.3 %reduce-scatter.21.cloned.1.call-start = ((), (), s32[]{:S(2)}) async-start(), calls=%async_computation.22 | async-start | bytes 5242880 | tf_op jit(solution)/shard_map/reduce_scatter | solution.py:186
  720.2 221.4 %reduce-scatter.19.cloned.1.call-start = ((), (), s32[]{:S(2)}) async-start(), calls=%async_computation.21 | async-start | bytes 10485760 | tf_op jit(solution)/shard_map/reduce_scatter | solution.py:186
  730.4 301.0 %reduce-scatter.17.cloned.1.call-start = ((), (), s32[]{:S(2)}) async-start(), calls=%async_computation.20 | async-start | bytes 10485760 | tf_op jit(solution)/shard_map/reduce_scatter | solution.py:186
  740.8 337.4 %reduce-scatter.11.cloned.1.call-start = ((), (), s32[]{:S(2)}) async-start(), calls=%async_computation.17 | async-start | bytes 3932160 | tf_op jit(solution)/shard_map/reduce_scatter | solution.py:186
  747.2 378.3 %reduce-scatter.9.cloned.1.call-start = ((), (), s32[]{:S(2)}) async-start(), calls=%async_computation.16 | async-start | bytes 3932160 | tf_op jit(solution)/shard_map/reduce_scatter | solution.py:186
  781.3 52.7 %collective-permute-start.33 = (bf16[64,2048]{1,0:T(8,128)(2,1)S(1)}, bf16[64,2048]{1,0:T(8,128)(2,1)}, u32[]{:S(2)}, u32[]{:S(2)}) collective-permute-start(bf16[64,2048]{1,0:T(8,128)(2,1)S(1)} %copy-done.40), channel_id=1, source_target_pairs={{0,8},{4,12},{8,0},{12,4},{1,9},{5,13},{9,1},{13,5},{2,10},{6,14},... | collective-permute-start | bytes 786440 | tf_op jit(solution)/shard_map/ppermute | solution.py:15
  786.5 47.6 %collective-permute-start.32 = (bf16[64,2048]{1,0:T(8,128)(2,1)S(1)}, bf16[64,2048]{1,0:T(8,128)(2,1)}, u32[]{:S(2)}, u32[]{:S(2)}) collective-permute-start(bf16[64,2048]{1,0:T(8,128)(2,1)S(1)} %copy-done.40), channel_id=1, source_target_pairs={{0,4},{4,0},{8,12},{12,8},{1,5},{5,1},{9,13},{13,9},{2,6},{6,2},{1... | collective-permute-start | bytes 786440 | tf_op jit(solution)/shard_map/ppermute | solution.py:15
  836.5 53.1 %collective-permute-start.35 = (bf16[4,64,2048]{2,1,0:T(8,128)(2,1)}, bf16[4,64,2048]{2,1,0:T(8,128)(2,1)}, u32[]{:S(2)}, u32[]{:S(2)}) collective-permute-start(bf16[4,64,2048]{2,1,0:T(8,128)(2,1)} %get-tuple-element.152), channel_id=1, source_target_pairs={{0,16},{16,0},{1,17},{17,1},{2,18},{18,2},{3,19},{19,3},{4,20},{20... | collective-permute-start | bytes 3145736 | tf_op jit(solution)/shard_map/ppermute | solution.py:15
  846.6 43.1 %collective-permute-start.67 = (bf16[4,64,2048]{2,1,0:T(8,128)(2,1)}, bf16[4,64,2048]{2,1,0:T(8,128)(2,1)}, u32[]{:S(2)}, u32[]{:S(2)}) collective-permute-start(bf16[4,64,2048]{2,1,0:T(8,128)(2,1)} %get-tuple-element.132), channel_id=1, source_target_pairs={{0,16},{16,0},{1,17},{17,1},{2,18},{18,2},{3,19},{19,3},{4,20},{20... | collective-permute-start | bytes 3145736 | tf_op jit(solution)/shard_map/ppermute | solution.py:15
  847.6 39.8 %collective-permute-start.69 = (bf16[256,512]{1,0:T(8,128)(2,1)S(1)}, bf16[256,512]{1,0:T(8,128)(2,1)S(1)}, u32[]{:S(2)}, u32[]{:S(2)}) collective-permute-start(bf16[256,512]{1,0:T(8,128)(2,1)S(1)} %broadcast_select_fusion.10), channel_id=1, source_target_pairs={{0,16},{16,0},{1,17},{17,1},{2,18},{18,2},{3,19},{19,3},{4,20},{20... | collective-permute-start | bytes 786440 | tf_op jit(solution)/shard_map/ppermute | solution.py:15
  898.6 234.7 %collective-permute-start.71 = (bf16[1024,512]{1,0:T(8,128)(2,1)}, bf16[1024,512]{1,0:T(8,128)(2,1)}, u32[]{:S(2)}, u32[]{:S(2)}) collective-permute-start(bf16[1024,512]{1,0:T(8,128)(2,1)} %broadcast_select_fusion.6), channel_id=1, source_target_pairs={{0,16},{16,0},{1,17},{17,1},{2,18},{18,2},{3,19},{19,3},{4,20},{20... | collective-permute-start | bytes 3145736 | tf_op jit(solution)/shard_map/ppermute | solution.py:15
  1038.0 106.8 %collective-permute-start.70 = (bf16[512,2,1024]{2,1,0:T(2,128)(2,1)}, bf16[512,2,1024]{2,1,0:T(2,128)(2,1)}, u32[]{:S(2)}, u32[]{:S(2)}) collective-permute-start(bf16[512,2,1024]{2,1,0:T(2,128)(2,1)} %select_n.320), channel_id=1, source_target_pairs={{0,16},{16,0},{1,17},{17,1},{2,18},{18,2},{3,19},{19,3},{4,20},{20... | collective-permute-start | bytes 6291464 | tf_op jit(solution)/shard_map/ppermute | solution.py:15
  (138 other events, 1967.3 us)
Sparse Core Ops, SparseCore 0:
  22.6 46.4 all-gather.10
  71.5 26.3 all-gather.12
  100.3 87.4 all-gather.14
  189.5 52.4 all-gather.16
  243.6 43.8 all-gather.18
  289.2 26.3 all-gather.20
  317.4 87.4 all-gather.22
  406.8 52.4 all-gather.24
  682.8 26.9 reduce-scatter.14
  712.5 27.9 reduce-scatter.12
  743.4 52.5 reduce-scatter.22
  798.9 52.5 reduce-scatter.20
  854.5 87.0 reduce-scatter.18
  945.1 86.2 reduce-scatter.16
  1034.2 43.8 reduce-scatter.10
  1081.6 43.8 reduce-scatter.8
